TPU v7x, 32 devices: a whole 2x2x4 slice. The times are simulated.
32 devices in a mesh: axial: 16 (over z, y, core), trans: 2 (over x).
Axes of the slice: x: 2, y: 2, z: 4, core: 2. Of those that a mesh axis runs over, the one named last changes fastest.
Arguments:
- source: float32 [128, 512, 512], P('axial', 'trans'), may hold values from -6 to 6
- labels: int32 [128, 512, 512], P('axial', 'trans'), may hold values from 0 to 3
- voltages: float32 [4], replicated, may hold values from -2 to 2
- relax: float32 [2, 512], replicated, may hold values from 0.3 to 1
Outputs:
- potential: float32 [128, 512, 512], P('axial', 'trans')
All inputs are finite; a program needn't handle non-finite values.
Results may differ from a plain program's by a relative error of at most 0.00008.
Values sent between devices are 32-bit elements; how exact they have to be, the bound alone decides.
No kernel may reach another device: no remote copies, remote signals or barrier semaphores. Data moves between devices by JAX's collectives and lax.ppermute only.
A program may use at most 128 MiB of HBM per device.

v0:
```python
import jax
import jax.numpy as jnp
from jax import lax
from jax.sharding import PartitionSpec as P

NX = 512
NY = 512


def from_partner(block, axis, bit):
    count = lax.axis_size(axis)
    route = []
    for low in range(count):
        high = low | 1 << bit
        if high != low and high < count:
            route += [(low, high), (high, low)]
    return lax.ppermute(block, axis, route)


def padded_2(shard, sides, width):
    for axis, dim in sides:
        count, length = (lax.axis_size(axis), shard.shape[dim])
        up = [(i, (i + 1) % count) for i in range(count - 1)]
        down = [(j, i) for i, j in up]
        last = lax.slice_in_dim(shard, length - width, length, axis=dim)
        initial = lax.slice_in_dim(shard, 0, width, axis=dim)
        before = lax.ppermute(last, axis, up)
        after = lax.ppermute(initial, axis, down)
        shard = jnp.concatenate([before, shard, after], axis=dim)
    return shard


def sine_table(count):
    index = jnp.arange(count, dtype=jnp.float32)
    scale = jnp.sqrt(2.0 / (count + 1.0))
    basis = scale * jnp.sin(
        jnp.pi * (index[:, None] + 1.0) * (index[None, :] + 1.0) / (count + 1.0)
    )
    eigen = 2.0 - 2.0 * jnp.cos(jnp.pi * (index + 1.0) / (count + 1.0))
    return (basis, eigen)


def mirror_in(slab):
    ax_count = lax.axis_size("axial")
    digits = ax_count.bit_length() - 1
    for bit in range(digits):
        slab = from_partner(slab, "axial", bit)
    return slab


def mirror_out(slab):
    ax_count = lax.axis_size("axial")
    digits = ax_count.bit_length() - 1
    for bit in range(digits):
        slab = from_partner(slab, "axial", bit)
    return slab


def on_device(source, labels, voltages, relax):
    high = lax.Precision.HIGHEST
    rows = source.shape[1]
    ax_count = lax.axis_size("axial")
    position = lax.axis_index("axial")
    lower = position < ax_count // 2
    basis_x, eigen_x = sine_table(NX)
    basis_y, eigen_y = sine_table(NY)
    row_start = lax.axis_index("trans") * rows
    columns = lax.dynamic_slice_in_dim(basis_x, row_start, rows, 1)
    charge = source
    for region in range(voltages.shape[0]):
        charge = charge + jnp.where(labels == region, voltages[region], 0.0)
    mirrored = mirror_in(charge)[::-1]
    folded = jnp.where(lower, 0.5 * (charge + mirrored), 0.5 * (charge - mirrored))
    inner = jnp.einsum("zxy,jy->zxj", folded, basis_y, precision=high)
    modes = lax.psum(jnp.einsum("kx,zxj->kzj", columns, inner, precision=high), "trans")
    weight_even = relax[0]
    weight_odd = relax[1]
    weight = jnp.where(lower, weight_even, weight_odd)[:, None, None]
    diag = eigen_x[:, None, None] + eigen_y[None, None, :] + 2.0
    first = weight * modes / diag
    padded = padded_2(first, (("axial", 1),), 1)
    below = padded[:, :-2]
    above = padded[:, 2:]
    second = first + weight * (modes - diag * first + below + above) / diag
    back = jnp.einsum("kzj,jy->kzy", second, basis_y, precision=high)
    field = jnp.einsum("kx,kzy->zxy", columns, back, precision=high)
    partner = mirror_out(field)[::-1]
    return field + jnp.where(lower, -1.0, 1.0) * partner


def solution(mesh):
    placed = (P("axial", "trans", None), P("axial", "trans", None), P(), P())
    return jax.shard_map(
        on_device, mesh=mesh, in_specs=placed, out_specs=P("axial", "trans", None), check_vma=False
    )
```

profile of v0, /device:TPU:0, one launch (start us, length us, event | category | flops | bytes accessed | tf_op | source)
XLA Modules:
  0.0 1099.4 jit_solution(4861309574738589126)
XLA Ops:
  6.5 0.0 all-reduce.2.cloned.1.call-start
  6.5 1.5 fusion.42
  8.0 6.9 select_add_fusion
  14.9 0.0 copy-start
  14.9 2.0 copy-done
  16.9 0.5 collective-permute-start
  17.4 6.8 collective-permute-done
  24.1 2.9 collective-permute-start.1
  27.0 90.9 %collective-permute-done.1 = f32[8,256,512]{2,1,0:T(8,128)S(1)} collective-permute-done((f32[8,256,512]{2,1,0:T(8,128)S(1)}, f32[8,256,512]{2,1,0:T(8,128)S(1)}, u32[]{:S(2)}, u32[]{:S(2)}) %collective-permute-start.1) | collective-permute-done | bytes 4194336 | tf_op jit(solution)/shard_map/ppermute | solution.py:17
  117.9 1.8 collective-permute-start.2
  119.7 90.4 %collective-permute-done.2 = f32[8,256,512]{2,1,0:T(8,128)} collective-permute-done((f32[8,256,512]{2,1,0:T(8,128)S(1)}, f32[8,256,512]{2,1,0:T(8,128)}, u32[]{:S(2)}, u32[]{:S(2)}) %collective-permute-start.2) | collective-permute-done | bytes 4194336 | tf_op jit(solution)/shard_map/ppermute | solution.py:17
  210.1 2.5 collective-permute-start.3
  212.6 3.6 sine_multiply_fusion
  216.2 176.2 %collective-permute-done.3 = f32[8,256,512]{2,1,0:T(8,128)} collective-permute-done((f32[8,256,512]{2,1,0:T(8,128)}, f32[8,256,512]{2,1,0:T(8,128)}, u32[]{:S(2)}, u32[]{:S(2)}) %collective-permute-start.3) | collective-permute-done | bytes 4194336 | tf_op jit(solution)/shard_map/ppermute | solution.py:17
  392.4 4.6 rev.6
  397.0 14.6 %fusion.8 = f32[8,256,512]{2,1,0:T(8,128)S(1)} fusion(f32[8,256,512]{2,1,0:T(8,128)} %copy-done, f32[8,256,512]{2,1,0:T(8,128)} %rev.6, pred[]{:T(512)S(6)} %lt.6, f32[512]{0:T(512)S(1)} %get-tuple-element.11, f32[512]{0:T(512)S(1)} %get-tuple-element.12), kind=kOutput, calls=%fused_computation.11 | convolution fusion | flops 6448480256 | bytes 12587009 | tf_op jit(solution)/shard_map/zxy,jy->zxj/dot_general | solution.py:74
  411.6 9.1 fusion.20
  420.7 0.0 copy-start.3
  420.7 0.0 all-reduce.2.cloned.1.call-update
  420.8 0.6 copy-done.3
  421.4 0.1 add_add_fusion
  421.5 198.1 %all-reduce.2.cloned.1.call-done = f32[512,8,512]{2,0,1:T(8,128)} async-done(((f32[512,8,512]{2,0,1:T(8,128)}), f32[512,8,512]{2,0,1:T(8,128)}) %all-reduce.2.cloned.1.call-update) | async-done | bytes 8388624 | tf_op jit(solution)/shard_map/psum | solution.py:75
  619.6 4.9 multiply_divide_fusion
  624.5 0.0 copy-start.2
  624.5 3.2 copy-done.2
  627.8 0.2 fusion.41
  627.9 1.8 collective-permute-start.4
  629.8 1.3 collective-permute-start.5
  631.1 0.9 collective-permute-done.4
  632.0 3.5 collective-permute-done.5
  635.5 40.0 %fusion.5 = f32[512,8,512]{0,2,1:T(8,128)} fusion(f32[512,8,512]{2,0,1:T(8,128)} %copy-done.2, f32[512,1,512]{2,0,1:T(8,128)S(1)} %collective-permute-done.5, f32[512,1,512]{2,0,1:T(8,128)S(1)} %collective-permute-done.4, f32[512,8,512]{2,0,1:T(8,128)} %all-reduce.2.cloned.1.call-done, f32[512,512]{1,0:T(8,128)S(1)} %add_add_fusion, f32[512]{0:T(512)S(1)} %bitcast.20, ...), kind=kOutput, calls=%fused_computation.8 | convolution fusion | flops 12904562688 | bytes 28317696 | tf_op jit(solution)/shard_map/kzj,jy->kzy/dot_general | solution.py:85
  675.5 9.2 convolution_bitcast_fusion
  684.6 0.0 copy-start.1
  684.6 2.0 copy-done.1
  686.6 18.9 %collective-permute-start.6 = (f32[8,256,512]{1,2,0:T(8,128)S(1)}, f32[8,256,512]{1,2,0:T(8,128)S(1)}, u32[]{:S(2)}, u32[]{:S(2)}) collective-permute-start(f32[8,256,512]{1,2,0:T(8,128)S(1)} %convolution_bitcast_fusion), channel_id=1, source_target_pairs={{0,2},{2,0},{4,6},{6,4},{8,10},{10,8},{12,14},{14,12},{16,18},{18,... | collective-permute-start | bytes 12582920 | tf_op jit(solution)/shard_map/ppermute | solution.py:17
  705.5 6.8 collective-permute-done.6
  712.3 2.7 collective-permute-start.7
  715.1 90.9 %collective-permute-done.7 = f32[8,256,512]{1,2,0:T(8,128)S(1)} collective-permute-done((f32[8,256,512]{1,2,0:T(8,128)S(1)}, f32[8,256,512]{1,2,0:T(8,128)S(1)}, u32[]{:S(2)}, u32[]{:S(2)}) %collective-permute-start.7) | collective-permute-done | bytes 4194336 | tf_op jit(solution)/shard_map/ppermute | solution.py:17
  805.9 2.3 collective-permute-start.8
  808.3 90.4 %collective-permute-done.8 = f32[8,256,512]{1,2,0:T(8,128)} collective-permute-done((f32[8,256,512]{1,2,0:T(8,128)S(1)}, f32[8,256,512]{1,2,0:T(8,128)}, u32[]{:S(2)}, u32[]{:S(2)}) %collective-permute-start.8) | collective-permute-done | bytes 4194336 | tf_op jit(solution)/shard_map/ppermute | solution.py:17
  898.7 2.7 collective-permute-start.9
  901.3 179.9 %collective-permute-done.9 = f32[8,256,512]{1,2,0:T(8,128)} collective-permute-done((f32[8,256,512]{1,2,0:T(8,128)}, f32[8,256,512]{1,2,0:T(8,128)}, u32[]{:S(2)}, u32[]{:S(2)}) %collective-permute-start.9) | collective-permute-done | bytes 4194336 | tf_op jit(solution)/shard_map/ppermute | solution.py:17
  1081.2 6.0 multiply_add_fusion
  1087.2 5.3 copy.5
  (3 shorter events, 0.1 us)
Async XLA Ops:
  6.5 613.1 %all-reduce.2.cloned.1.call-start = ((), (), s32[]{:S(2)}) async-start(), calls=%async_computation | async-start | bytes 16777216 | tf_op jit(solution)/shard_map/psum | solution.py:75
  14.9 2.0 copy-start
  16.9 7.2 collective-permute-start
  24.1 93.8 %collective-permute-start.1 = (f32[8,256,512]{2,1,0:T(8,128)S(1)}, f32[8,256,512]{2,1,0:T(8,128)S(1)}, u32[]{:S(2)}, u32[]{:S(2)}) collective-permute-start(f32[8,256,512]{2,1,0:T(8,128)S(1)} %collective-permute-done), channel_id=1, source_target_pairs={{0,4},{4,0},{2,6},{6,2},{8,12},{12,8},{10,14},{14,10},{16,20},{20,... | collective-permute-start | bytes 12582920 | tf_op jit(solution)/shard_map/ppermute | solution.py:17
  117.9 92.2 %collective-permute-start.2 = (f32[8,256,512]{2,1,0:T(8,128)S(1)}, f32[8,256,512]{2,1,0:T(8,128)}, u32[]{:S(2)}, u32[]{:S(2)}) collective-permute-start(f32[8,256,512]{2,1,0:T(8,128)S(1)} %collective-permute-done.1), channel_id=1, source_target_pairs={{0,8},{8,0},{2,10},{10,2},{4,12},{12,4},{6,14},{14,6},{16,24},{24,... | collective-permute-start | bytes 12582920 | tf_op jit(solution)/shard_map/ppermute | solution.py:17
  210.1 182.3 %collective-permute-start.3 = (f32[8,256,512]{2,1,0:T(8,128)}, f32[8,256,512]{2,1,0:T(8,128)}, u32[]{:S(2)}, u32[]{:S(2)}) collective-permute-start(f32[8,256,512]{2,1,0:T(8,128)} %collective-permute-done.2), channel_id=1, source_target_pairs={{0,16},{16,0},{2,18},{18,2},{4,20},{20,4},{6,22},{22,6},{8,24},{24... | collective-permute-start | bytes 12582920 | tf_op jit(solution)/shard_map/ppermute | solution.py:17
  420.7 0.7 copy-start.3
  624.5 3.2 copy-start.2
  627.9 4.0 collective-permute-start.4
  629.8 5.7 collective-permute-start.5
  684.6 2.0 copy-start.1
  686.6 25.7 %collective-permute-start.6 = (f32[8,256,512]{1,2,0:T(8,128)S(1)}, f32[8,256,512]{1,2,0:T(8,128)S(1)}, u32[]{:S(2)}, u32[]{:S(2)}) collective-permute-start(f32[8,256,512]{1,2,0:T(8,128)S(1)} %convolution_bitcast_fusion), channel_id=1, source_target_pairs={{0,2},{2,0},{4,6},{6,4},{8,10},{10,8},{12,14},{14,12},{16,18},{18,... | collective-permute-start | bytes 12582920 | tf_op jit(solution)/shard_map/ppermute | solution.py:17
  712.3 93.6 %collective-permute-start.7 = (f32[8,256,512]{1,2,0:T(8,128)S(1)}, f32[8,256,512]{1,2,0:T(8,128)S(1)}, u32[]{:S(2)}, u32[]{:S(2)}) collective-permute-start(f32[8,256,512]{1,2,0:T(8,128)S(1)} %collective-permute-done.6), channel_id=1, source_target_pairs={{0,4},{4,0},{2,6},{6,2},{8,12},{12,8},{10,14},{14,10},{16,20},{20,... | collective-permute-start | bytes 12582920 | tf_op jit(solution)/shard_map/ppermute | solution.py:17
  805.9 92.7 %collective-permute-start.8 = (f32[8,256,512]{1,2,0:T(8,128)S(1)}, f32[8,256,512]{1,2,0:T(8,128)}, u32[]{:S(2)}, u32[]{:S(2)}) collective-permute-start(f32[8,256,512]{1,2,0:T(8,128)S(1)} %collective-permute-done.7), channel_id=1, source_target_pairs={{0,8},{8,0},{2,10},{10,2},{4,12},{12,4},{6,14},{14,6},{16,24},{24,... | collective-permute-start | bytes 12582920 | tf_op jit(solution)/shard_map/ppermute | solution.py:17
  898.7 182.5 %collective-permute-start.9 = (f32[8,256,512]{1,2,0:T(8,128)}, f32[8,256,512]{1,2,0:T(8,128)}, u32[]{:S(2)}, u32[]{:S(2)}) collective-permute-start(f32[8,256,512]{1,2,0:T(8,128)} %collective-permute-done.8), channel_id=1, source_target_pairs={{0,16},{16,0},{2,18},{18,2},{4,20},{20,4},{6,22},{22,6},{8,24},{24... | collective-permute-start | bytes 12582920 | tf_op jit(solution)/shard_map/ppermute | solution.py:17
Sparse Core Ops, SparseCore 0:
  420.8 198.7 all-reduce.1
where the time goes:
time: 1100 us
  waiting for transfers between devices  935 us (85%)
  matrix products  72.8 us (7%)
  starting transfers between devices  37.4 us (3%)
  other arithmetic  21.5 us (2%)
  local copies, waits for them, and re-layouts  19.4 us (2%)
  between operations  13.5 us (1%)
    ppermute x8, waiting for transfers between devices, from_partner(): return lax.ppermute(block, axis, route)  732 us
    psum x1, waiting for transfers between devices, on_device(): lax.psum(jnp.einsum('kx,zxj->kzj', columns, inner, precision=high), 'trans')  198 us
    dot_general x1, matrix products, on_device(): back = jnp.einsum('kzj,jy->kzy', second, basis_y, precision=high)  40 us
    ppermute x8, starting transfers between devices, from_partner(): return lax.ppermute(block, axis, route)  34.3 us
  transfers between devices with their start and end apart: 11, of which 11 were waited for; matrix products, arithmetic and copies ran while one was open for 0% of the time, Pallas kernels for 0%

commit v1 on v0

--- a/solution.py
+++ b/solution.py
@@ -72,7 +72,9 @@
     mirrored = mirror_in(charge)[::-1]
     folded = jnp.where(lower, 0.5 * (charge + mirrored), 0.5 * (charge - mirrored))
     inner = jnp.einsum("zxy,jy->zxj", folded, basis_y, precision=high)
-    modes = lax.psum(jnp.einsum("kx,zxj->kzj", columns, inner, precision=high), "trans")
+    modes = jnp.sum(
+        lax.all_gather(jnp.einsum("kx,zxj->kzj", columns, inner, precision=high), "trans"), axis=0
+    )
     weight_even = relax[0]
     weight_odd = relax[1]
     weight = jnp.where(lower, weight_even, weight_odd)[:, None, None]

time: 1100 us -> 1120 us (1.018)
  other arithmetic: 21.5 us -> 33.6 us
    all_gather x0 -> x1, waiting for transfers between devices: none -> 199 us  [on_device(): lax.all_gather(jnp.einsum('kx,zxj->kzj', columns, inner, precision=high),...]
    psum x1 -> x0, waiting for transfers between devices: 198 us -> none  [on_device(): lax.psum(jnp.einsum('kx,zxj->kzj', columns, inner, precision=high), 'trans')]
    reduce_sum x0 -> x1, other arithmetic: none -> 12.1 us  [on_device(): jnp.sum(lax.all_gather(jnp.einsum('kx,zxj->kzj', columns, inner, precisio...]
where the time goes in v1:
time: 1120 us; the launch traced here: 1110 us
  waiting for transfers between devices  936 us (84%)
  matrix products  73.4 us (7%)
  starting transfers between devices  37.4 us (3%)
  other arithmetic  33.6 us (3%)
  local copies, waits for them, and re-layouts  19.4 us (2%)
  between operations  13.7 us (1%)
    ppermute x8, waiting for transfers between devices, from_partner(): return lax.ppermute(block, axis, route)  732 us
    all_gather x1, waiting for transfers between devices, on_device(): lax.all_gather(jnp.einsum('kx,zxj->kzj', columns, inner, precision=high),...  199 us
    dot_general x1, matrix products, on_device(): back = jnp.einsum('kzj,jy->kzy', second, basis_y, precision=high)  40 us
    ppermute x8, starting transfers between devices, from_partner(): return lax.ppermute(block, axis, route)  34.3 us
  transfers between devices with their start and end apart: 11, of which 11 were waited for; matrix products, arithmetic and copies ran while one was open for 0% of the time, Pallas kernels for 0%

profile of v1, /device:TPU:0, one launch (start us, length us, event | category | flops | bytes accessed | tf_op | source)
XLA Modules:
  0.0 1113.1 jit_solution(3405950624693349783)
XLA Ops:
  6.5 0.0 all-gather.3.cloned.1.call-start
  6.5 1.5 fusion.42
  8.0 6.9 select_add_fusion
  14.9 0.0 copy-start
  14.9 2.0 copy-done
  16.9 0.5 collective-permute-start
  17.4 6.8 collective-permute-done
  24.1 2.9 collective-permute-start.1
  27.0 90.9 %collective-permute-done.1 = f32[8,256,512]{2,1,0:T(8,128)S(1)} collective-permute-done((f32[8,256,512]{2,1,0:T(8,128)S(1)}, f32[8,256,512]{2,1,0:T(8,128)S(1)}, u32[]{:S(2)}, u32[]{:S(2)}) %collective-permute-start.1) | collective-permute-done | bytes 4194336 | tf_op jit(solution)/shard_map/ppermute | solution.py:17
  117.9 1.8 collective-permute-start.2
  119.7 90.4 %collective-permute-done.2 = f32[8,256,512]{2,1,0:T(8,128)} collective-permute-done((f32[8,256,512]{2,1,0:T(8,128)S(1)}, f32[8,256,512]{2,1,0:T(8,128)}, u32[]{:S(2)}, u32[]{:S(2)}) %collective-permute-start.2) | collective-permute-done | bytes 4194336 | tf_op jit(solution)/shard_map/ppermute | solution.py:17
  210.1 2.5 collective-permute-start.3
  212.6 3.6 sine_multiply_fusion
  216.2 176.2 %collective-permute-done.3 = f32[8,256,512]{2,1,0:T(8,128)} collective-permute-done((f32[8,256,512]{2,1,0:T(8,128)}, f32[8,256,512]{2,1,0:T(8,128)}, u32[]{:S(2)}, u32[]{:S(2)}) %collective-permute-start.3) | collective-permute-done | bytes 4194336 | tf_op jit(solution)/shard_map/ppermute | solution.py:17
  392.4 4.6 rev.6
  397.0 14.8 %fusion.8 = f32[8,256,512]{2,1,0:T(8,128)S(1)} fusion(f32[8,256,512]{2,1,0:T(8,128)} %copy-done, f32[8,256,512]{2,1,0:T(8,128)} %rev.6, pred[]{:T(512)S(6)} %lt.6, f32[512]{0:T(512)S(1)} %get-tuple-element.11, f32[512]{0:T(512)S(1)} %get-tuple-element.12), kind=kOutput, calls=%fused_computation.11 | convolution fusion | flops 6448480256 | bytes 12587009 | tf_op jit(solution)/shard_map/zxy,jy->zxj/dot_general | solution.py:74
  411.9 9.2 fusion.20
  421.1 0.0 copy-start.3
  421.1 0.0 all-gather.3.cloned.1.call-update
  421.1 0.6 copy-done.3
  421.8 0.1 add_add_fusion
  421.9 198.9 %all-gather.3.cloned.1.call-done = f32[1024,8,512]{2,0,1:T(8,128)} async-done(((f32[512,8,512]{2,0,1:T(8,128)}), f32[1024,8,512]{2,0,1:T(8,128)}) %all-gather.3.cloned.1.call-update) | async-done | bytes 16777232 | tf_op jit(solution)/shard_map/all_gather | solution.py:76
  620.8 12.1 %reduce_sum.9 = f32[512,8,512]{2,0,1:T(8,128)} reduce(f32[2,512,8,512]{3,1,0,2:T(8,128)} %bitcast.20, f32[]{:T(128)} %constant.10.clone.1), dimensions={0}, to_apply=%region_0.1 | reduce | flops 2097152 | bytes 25165828 | tf_op jit(solution)/shard_map/reduce_sum | solution.py:75
  632.9 4.9 multiply_divide_fusion
  637.8 0.0 copy-start.2
  637.8 3.2 copy-done.2
  641.0 0.2 fusion.41
  641.2 1.8 collective-permute-start.4
  643.0 1.3 collective-permute-start.5
  644.3 0.9 collective-permute-done.4
  645.2 3.5 collective-permute-done.5
  648.8 40.0 %fusion.5 = f32[512,8,512]{0,2,1:T(8,128)} fusion(f32[512,8,512]{2,0,1:T(8,128)} %copy-done.2, f32[512,1,512]{2,0,1:T(8,128)S(1)} %collective-permute-done.5, f32[512,1,512]{2,0,1:T(8,128)S(1)} %collective-permute-done.4, f32[512,8,512]{2,0,1:T(8,128)} %reduce_sum.9, f32[512,512]{1,0:T(8,128)S(1)} %add_add_fusion, f32[512]{0:T(512)S(1)} %bitcast.22, ...), kind=kOutput, calls=%fused_computation.8 | convolution fusion | flops 12904562688 | bytes 28317696 | tf_op jit(solution)/shard_map/kzj,jy->kzy/dot_general | solution.py:87
  688.7 9.3 convolution_bitcast_fusion
  698.1 0.0 copy-start.1
  698.1 2.0 copy-done.1
  700.1 18.9 %collective-permute-start.6 = (f32[8,256,512]{1,2,0:T(8,128)S(1)}, f32[8,256,512]{1,2,0:T(8,128)S(1)}, u32[]{:S(2)}, u32[]{:S(2)}) collective-permute-start(f32[8,256,512]{1,2,0:T(8,128)S(1)} %convolution_bitcast_fusion), channel_id=1, source_target_pairs={{0,2},{2,0},{4,6},{6,4},{8,10},{10,8},{12,14},{14,12},{16,18},{18,... | collective-permute-start | bytes 12582920 | tf_op jit(solution)/shard_map/ppermute | solution.py:17
  719.0 6.8 collective-permute-done.6
  725.8 2.7 collective-permute-start.7
  728.5 90.9 %collective-permute-done.7 = f32[8,256,512]{1,2,0:T(8,128)S(1)} collective-permute-done((f32[8,256,512]{1,2,0:T(8,128)S(1)}, f32[8,256,512]{1,2,0:T(8,128)S(1)}, u32[]{:S(2)}, u32[]{:S(2)}) %collective-permute-start.7) | collective-permute-done | bytes 4194336 | tf_op jit(solution)/shard_map/ppermute | solution.py:17
  819.4 2.3 collective-permute-start.8
  821.7 90.4 %collective-permute-done.8 = f32[8,256,512]{1,2,0:T(8,128)} collective-permute-done((f32[8,256,512]{1,2,0:T(8,128)S(1)}, f32[8,256,512]{1,2,0:T(8,128)}, u32[]{:S(2)}, u32[]{:S(2)}) %collective-permute-start.8) | collective-permute-done | bytes 4194336 | tf_op jit(solution)/shard_map/ppermute | solution.py:17
  912.1 2.7 collective-permute-start.9
  914.8 179.9 %collective-permute-done.9 = f32[8,256,512]{1,2,0:T(8,128)} collective-permute-done((f32[8,256,512]{1,2,0:T(8,128)}, f32[8,256,512]{1,2,0:T(8,128)}, u32[]{:S(2)}, u32[]{:S(2)}) %collective-permute-start.9) | collective-permute-done | bytes 4194336 | tf_op jit(solution)/shard_map/ppermute | solution.py:17
  1094.7 6.0 multiply_add_fusion
  1100.6 5.3 copy.6
  (3 shorter events, 0.1 us)
Async XLA Ops:
  6.5 614.3 %all-gather.3.cloned.1.call-start = ((), (), s32[]{:S(2)}) async-start(), calls=%async_computation | async-start | bytes 25165824 | tf_op jit(solution)/shard_map/all_gather | solution.py:76
  14.9 2.0 copy-start
  16.9 7.2 collective-permute-start
  24.1 93.8 %collective-permute-start.1 = (f32[8,256,512]{2,1,0:T(8,128)S(1)}, f32[8,256,512]{2,1,0:T(8,128)S(1)}, u32[]{:S(2)}, u32[]{:S(2)}) collective-permute-start(f32[8,256,512]{2,1,0:T(8,128)S(1)} %collective-permute-done), channel_id=1, source_target_pairs={{0,4},{4,0},{2,6},{6,2},{8,12},{12,8},{10,14},{14,10},{16,20},{20,... | collective-permute-start | bytes 12582920 | tf_op jit(solution)/shard_map/ppermute | solution.py:17
  117.9 92.2 %collective-permute-start.2 = (f32[8,256,512]{2,1,0:T(8,128)S(1)}, f32[8,256,512]{2,1,0:T(8,128)}, u32[]{:S(2)}, u32[]{:S(2)}) collective-permute-start(f32[8,256,512]{2,1,0:T(8,128)S(1)} %collective-permute-done.1), channel_id=1, source_target_pairs={{0,8},{8,0},{2,10},{10,2},{4,12},{12,4},{6,14},{14,6},{16,24},{24,... | collective-permute-start | bytes 12582920 | tf_op jit(solution)/shard_map/ppermute | solution.py:17
  210.1 182.3 %collective-permute-start.3 = (f32[8,256,512]{2,1,0:T(8,128)}, f32[8,256,512]{2,1,0:T(8,128)}, u32[]{:S(2)}, u32[]{:S(2)}) collective-permute-start(f32[8,256,512]{2,1,0:T(8,128)} %collective-permute-done.2), channel_id=1, source_target_pairs={{0,16},{16,0},{2,18},{18,2},{4,20},{20,4},{6,22},{22,6},{8,24},{24... | collective-permute-start | bytes 12582920 | tf_op jit(solution)/shard_map/ppermute | solution.py:17
  421.1 0.7 copy-start.3
  637.8 3.2 copy-start.2
  641.2 4.0 collective-permute-start.4
  643.0 5.7 collective-permute-start.5
  698.1 2.0 copy-start.1
  700.1 25.7 %collective-permute-start.6 = (f32[8,256,512]{1,2,0:T(8,128)S(1)}, f32[8,256,512]{1,2,0:T(8,128)S(1)}, u32[]{:S(2)}, u32[]{:S(2)}) collective-permute-start(f32[8,256,512]{1,2,0:T(8,128)S(1)} %convolution_bitcast_fusion), channel_id=1, source_target_pairs={{0,2},{2,0},{4,6},{6,4},{8,10},{10,8},{12,14},{14,12},{16,18},{18,... | collective-permute-start | bytes 12582920 | tf_op jit(solution)/shard_map/ppermute | solution.py:17
  725.8 93.6 %collective-permute-start.7 = (f32[8,256,512]{1,2,0:T(8,128)S(1)}, f32[8,256,512]{1,2,0:T(8,128)S(1)}, u32[]{:S(2)}, u32[]{:S(2)}) collective-permute-start(f32[8,256,512]{1,2,0:T(8,128)S(1)} %collective-permute-done.6), channel_id=1, source_target_pairs={{0,4},{4,0},{2,6},{6,2},{8,12},{12,8},{10,14},{14,10},{16,20},{20,... | collective-permute-start | bytes 12582920 | tf_op jit(solution)/shard_map/ppermute | solution.py:17
  819.4 92.7 %collective-permute-start.8 = (f32[8,256,512]{1,2,0:T(8,128)S(1)}, f32[8,256,512]{1,2,0:T(8,128)}, u32[]{:S(2)}, u32[]{:S(2)}) collective-permute-start(f32[8,256,512]{1,2,0:T(8,128)S(1)} %collective-permute-done.7), channel_id=1, source_target_pairs={{0,8},{8,0},{2,10},{10,2},{4,12},{12,4},{6,14},{14,6},{16,24},{24,... | collective-permute-start | bytes 12582920 | tf_op jit(solution)/shard_map/ppermute | solution.py:17
  912.1 182.5 %collective-permute-start.9 = (f32[8,256,512]{1,2,0:T(8,128)}, f32[8,256,512]{1,2,0:T(8,128)}, u32[]{:S(2)}, u32[]{:S(2)}) collective-permute-start(f32[8,256,512]{1,2,0:T(8,128)} %collective-permute-done.8), channel_id=1, source_target_pairs={{0,16},{16,0},{2,18},{18,2},{4,20},{20,4},{6,22},{22,6},{8,24},{24... | collective-permute-start | bytes 12582920 | tf_op jit(solution)/shard_map/ppermute | solution.py:17
Sparse Core Ops, SparseCore 0:
  421.2 199.5 all-gather.2
